TPU v7x, 32 devices: a whole 2x2x4 slice. The times are simulated.
32 devices in a mesh: pages: 2 (over y), tile: 4 (over z), mp: 2 (over x), batch: 2 (over core).
Axes of the slice: x: 2, y: 2, z: 4, core: 2. Of those that a mesh axis runs over, the one named last changes fastest.
Arguments:
- page_cells: bfloat16 [4, 48, 24, 1024], P(('pages', 'batch'), 'tile'), parts along dimension 0, may hold values from -40 to 40
- text_states: bfloat16 [4, 1024, 1024], P(('pages', 'batch'), 'tile'), parts along dimension 0, may hold values from -40 to 40
- enc_query: bfloat16 [1024, 1024], P('batch', 'mp'), may hold values from -2.5 to 2.5
- enc_keyval: bfloat16 [1024, 2, 1024], P('batch', None, 'mp'), may hold values from -0.1875 to 0.1875
- enc_proj: bfloat16 [1024, 1024], P('mp', 'batch'), may hold values from -0.1875 to 0.1875
- dec_query: bfloat16 [1024, 1024], P('batch', 'mp'), may hold values from -2.5 to 2.5
- dec_keyval: bfloat16 [1024, 2, 1024], P('batch', None, 'mp'), may hold values from -0.1875 to 0.1875
- dec_out: bfloat16 [1024, 1024], P('mp', 'batch'), may hold values from -0.1875 to 0.1875
Outputs:
- encoded: bfloat16 [4, 48, 24, 1024], P(('pages', 'batch'), 'tile'), parts along dimension 0
- decoded: bfloat16 [4, 1024, 1024], P(('pages', 'batch'), ('tile', 'mp')), parts along dimension 0
There are 2 independent parts, one for each index of `pages`. A program takes and returns all parts, laid end to end along the dimension named above; an argument that names none is the same for every part. Nothing has to cross between parts.
All inputs are finite; a program needn't handle non-finite values.
Results may differ from a plain program's by a relative error of at most 0.012.
Values may be sent and summed in bfloat16 or wider, within the bound.
No kernel may reach another device: no remote copies, remote signals or barrier semaphores. Data moves between devices by JAX's collectives and lax.ppermute only.
A program may use at most 64 MiB of HBM per device.

v0:
```python
import math
import jax
import jax.numpy as jnp
from jax import lax
from jax.sharding import PartitionSpec as P

HEAD_ENC = 32
HEAD_DEC = 64


def from_behind(value, axis, by):
    devices = lax.axis_size(axis)
    return lax.ppermute(value, axis, [(i, (i + by) % devices) for i in range(devices)])


def layer_norm(values):
    center = values - jnp.mean(values, axis=-1, keepdims=True)
    variance = jnp.mean(center * center, axis=-1, keepdims=True)
    return center / jnp.sqrt(variance + 1e-05)


def regions(length, window, offset):
    index_row = jnp.arange(length, dtype=jnp.int32)
    return jnp.where(
        index_row < length - window, 0, jnp.where(index_row < length - offset, 1, 2)
    ).astype(jnp.int32)


def body(page_cells, text_states, enc_query, enc_keyval, enc_proj, dec_query, dec_keyval, dec_out):
    wq_enc, wkv_enc, wproj_enc, wq_dec, wkv_dec, wout_dec = (
        lax.all_gather(enc_query, "batch", axis=0, tiled=True),
        lax.all_gather(enc_keyval, "batch", axis=0, tiled=True),
        lax.all_gather(enc_proj, "batch", axis=1, tiled=True),
        lax.all_gather(dec_query, "batch", axis=0, tiled=True),
        lax.all_gather(dec_keyval, "batch", axis=0, tiled=True),
        lax.all_gather(dec_out, "batch", axis=1, tiled=True),
    )
    pages_here, window, columns, width = page_cells.shape
    offset = window // 2
    own_rows = window * columns
    hq_enc = wq_enc.shape[1]
    heads_enc = hq_enc // HEAD_ENC
    joined = jnp.concatenate([wq_enc, wkv_enc.reshape(width, 2 * hq_enc)], axis=1)
    rows_below = from_behind(page_cells[:, :offset], "tile", -1)
    normed = layer_norm(
        jnp.concatenate([page_cells[:, offset:], rows_below], axis=1).astype(jnp.float32)
    ).astype(jnp.bfloat16)
    projected = jnp.einsum(
        "prcd,de->prce", normed, joined, preferred_element_type=jnp.float32
    ).astype(jnp.bfloat16)
    projected = jnp.roll(projected, -offset, axis=2)
    per_row = columns // window
    shaped = projected.reshape(pages_here, window, per_row, window, 3, heads_enc, HEAD_ENC)
    shaped = jnp.swapaxes(shaped, 1, 2).reshape(
        pages_here, per_row, window * window, 3, heads_enc, HEAD_ENC
    )
    win_q = shaped[:, :, :, 0]
    win_k = shaped[:, :, :, 1]
    win_v = shaped[:, :, :, 2]
    is_last = lax.axis_index("tile") == lax.axis_size("tile") - 1
    local_rows = jnp.arange(window, dtype=jnp.int32)
    row_region = jnp.where(is_last, jnp.where(local_rows < window - offset, 1, 2), 0).astype(
        jnp.int32
    )
    labels = row_region[:, None] * 3 + regions(columns, window, offset)[None, :]
    labels = jnp.swapaxes(labels.reshape(window, per_row, window), 0, 1).reshape(
        per_row, window * window
    )
    allowed = labels[:, :, None] == labels[:, None, :]
    win_scores = jnp.einsum(
        "pnqhd,pnkhd->pnhqk", win_q, win_k, preferred_element_type=jnp.float32
    ) / math.sqrt(HEAD_ENC)
    win_scores = jnp.where(allowed[None, :, None], win_scores, -jnp.inf)
    top = jnp.max(win_scores, axis=-1, keepdims=True)
    expd = jnp.exp(win_scores - top)
    win_weights = (expd / jnp.sum(expd, axis=-1, keepdims=True)).astype(jnp.bfloat16)
    win_out = jnp.einsum(
        "pnhqk,pnkhd->pnqhd", win_weights, win_v, preferred_element_type=jnp.float32
    ).astype(jnp.bfloat16)
    win_out = win_out.reshape(pages_here, per_row, window, window, hq_enc)
    win_out = jnp.swapaxes(win_out, 1, 2).reshape(pages_here, window, columns, hq_enc)
    win_out = jnp.roll(win_out, offset, axis=2)
    rows_above = from_behind(win_out[:, window - offset :], "tile", 1)
    unrolled = jnp.concatenate([rows_above, win_out[:, : window - offset]], axis=1)
    partial_proj = jnp.einsum(
        "prce,ed->prcd", unrolled, wproj_enc, preferred_element_type=jnp.float32
    )
    summed = lax.psum(partial_proj.astype(jnp.bfloat16), "mp").astype(jnp.float32)
    encoded = (page_cells.astype(jnp.float32) + summed).astype(jnp.bfloat16)
    hq_dec = wq_dec.shape[1]
    heads_dec = hq_dec // HEAD_DEC
    page_normed = (
        layer_norm(encoded.astype(jnp.float32))
        .astype(jnp.bfloat16)
        .reshape(pages_here, own_rows, width)
    )
    page_kv = jnp.einsum(
        "pnd,de->pne",
        page_normed,
        wkv_dec.reshape(width, 2 * hq_dec),
        preferred_element_type=jnp.float32,
    ).astype(jnp.bfloat16)
    text_normed = layer_norm(text_states.astype(jnp.float32)).astype(jnp.bfloat16)
    queries = jnp.einsum(
        "ptd,de->pte", text_normed, wq_dec, preferred_element_type=jnp.float32
    ).astype(jnp.bfloat16)
    text_len = text_states.shape[1]
    query_heads = queries.reshape(pages_here, text_len, heads_dec, HEAD_DEC)
    start_state = (
        jnp.full((pages_here, heads_dec, text_len), -jnp.inf, jnp.float32),
        jnp.zeros((pages_here, heads_dec, text_len), jnp.float32),
        jnp.zeros((pages_here, heads_dec, text_len, HEAD_DEC), jnp.float32),
    )
    carried = start_state
    shard_rows = lax.all_gather(page_kv, "tile", axis=1, tiled=True)
    count = shard_rows.shape[1] // own_rows
    grouped = max(
        (
            factor
            for factor in range(1, count + 1)
            if count % factor == 0 and factor * own_rows <= 2048
        )
    )
    blocks = jnp.moveaxis(
        shard_rows.reshape(pages_here, count // grouped, grouped * own_rows, 2 * hq_dec), 1, 0
    )

    def advance(running, block_kv):
        maxima, totals, accum = running
        span = block_kv.shape[1]
        block_keys = block_kv[..., :hq_dec].reshape(pages_here, span, heads_dec, HEAD_DEC)
        block_vals = block_kv[..., hq_dec:].reshape(pages_here, span, heads_dec, HEAD_DEC)
        cross_scores = jnp.einsum(
            "pqhd,pkhd->phqk", query_heads, block_keys, preferred_element_type=jnp.float32
        ) / math.sqrt(HEAD_DEC)
        newest = jnp.maximum(maxima, jnp.max(cross_scores, axis=-1))
        rescale = jnp.exp(maxima - newest)
        expo = jnp.exp(cross_scores - newest[..., None])
        totals = totals * rescale + jnp.sum(expo, axis=-1)
        accum = accum * rescale[..., None] + jnp.einsum(
            "phqk,pkhd->phqd",
            expo.astype(jnp.bfloat16),
            block_vals,
            preferred_element_type=jnp.float32,
        )
        return ((newest, totals, accum), None)

    carried, unused = lax.scan(advance, carried, blocks)
    maxima, totals, accum = carried
    context = (
        jnp.transpose(accum / totals[..., None], (0, 2, 1, 3))
        .reshape(pages_here, text_len, hq_dec)
        .astype(jnp.bfloat16)
    )
    share = text_len // lax.axis_size("mp")
    mixed = lax.psum_scatter(
        jnp.einsum("pte,ed->tpd", context, wout_dec, preferred_element_type=jnp.float32).astype(
            jnp.bfloat16
        ),
        "mp",
        scatter_dimension=0,
        tiled=True,
    ).astype(jnp.float32)
    own_text = lax.dynamic_slice_in_dim(text_states, lax.axis_index("mp") * share, share, 1)
    decoded = (own_text.astype(jnp.float32) + jnp.moveaxis(mixed, 0, 1)).astype(jnp.bfloat16)
    return (encoded, decoded)


def solution(mesh):
    placed = (
        P(("pages", "batch"), "tile", None, None),
        P(("pages", "batch"), "tile", None),
        P("batch", "mp"),
        P("batch", None, "mp"),
        P("mp", "batch"),
        P("batch", "mp"),
        P("batch", None, "mp"),
        P("mp", "batch"),
    )
    return jax.shard_map(
        body,
        mesh=mesh,
        in_specs=placed,
        out_specs=(
            P(("pages", "batch"), "tile", None, None),
            P(("pages", "batch"), ("tile", "mp"), None),
        ),
        check_vma=False,
    )
```

profile of v0, /device:TPU:0, one launch (start us, length us, event | category | flops | bytes accessed | tf_op | source)
XLA Modules:
  0.0 199.5 jit_solution(16749749369688853707)
XLA Ops:
  7.2 0.7 all-gather.11.cloned.1.call-update
  7.9 0.0 all-gather.9.cloned.1.call-start
  8.0 0.7 all-gather.9.cloned.1.call-update
  8.7 0.7 all-gather.13.cloned.1.call-update
  9.4 0.1 fusion.80
  9.6 5.1 %collective-permute-start = (bf16[1,6,24,1024]{3,2,1,0:T(8,128)(2,1)S(1)}, bf16[1,6,24,1024]{3,2,1,0:T(8,128)(2,1)S(1)}, u32[]{:S(2)}, u32[]{:S(2)}) collective-permute-start(bf16[1,6,24,1024]{3,2,1,0:T(8,128)(2,1)S(1)} %get-tuple-element.29), channel_id=1, source_target_pairs={{0,12},{4,0},{8,4},{12,8},{1,13},{5,1},{9,5},{13,9},{2,14},{6,2},{... | collective-permute-start | bytes 884744 | tf_op jit(solution)/shard_map/ppermute | solution.py:13
  14.7 0.0 all-reduce.2.cloned.1.call-start
  14.8 0.1 add.86
  14.9 0.1 add.82
  14.9 0.1 add.83
  15.0 0.7 broadcast_compare_fusion
  15.8 5.1 %collective-permute-done = bf16[1,6,24,1024]{3,2,1,0:T(8,128)(2,1)S(1)} collective-permute-done((bf16[1,6,24,1024]{3,2,1,0:T(8,128)(2,1)S(1)}, bf16[1,6,24,1024]{3,2,1,0:T(8,128)(2,1)S(1)}, u32[]{:S(2)}, u32[]{:S(2)}) %collective-permute-start) | collective-permute-done | bytes 294944 | tf_op jit(solution)/shard_map/ppermute | solution.py:13
  20.9 0.1 convert_reduce_fusion.1
  21.1 0.3 fusion.31
  21.4 1.5 all-gather.11.cloned.1.call-done
  22.9 2.1 %copy.40 = bf16[128,8,2,512]{3,1,2,0:T(8,128)(2,1)S(1)} copy(bf16[128,8,2,512]{3,2,1,0:T(2,128)(2,1)} %bitcast.102) | data formatting | bytes 4194304
  25.1 9.6 %all-gather.9.cloned.1.call-done = bf16[1024,512]{1,0:T(8,128)(2,1)} async-done(((bf16[512,512]{1,0:T(8,128)(2,1)}), bf16[1024,512]{1,0:T(8,128)(2,1)}) %all-gather.9.cloned.1.call-update) | async-done | bytes 1048592 | tf_op jit(solution)/shard_map/all_gather | solution.py:31
  34.7 2.4 %fusion.12 = bf16[1,12,24,1536]{3,2,1,0:T(8,128)(2,1)S(1)} fusion(bf16[1024,1024]{1,0:T(8,128)(2,1)S(1)} %bitcast.104, bf16[1024,512]{1,0:T(8,128)(2,1)} %all-gather.9.cloned.1.call-done, bf16[6,24,1024]{2,1,0:T(8,128)(2,1)S(1)} %bitcast.106, bf16[6,24,1024]{2,1,0:T(8,128)(2,1)S(1)} %get-tuple-element.28, f32[12,24]{1,0:T(8,128)S(1)} %add_sqrt_fusion.1, ...), kind=kOutput, calls=%fused_computation.17 | convolution fusion | flops 914178048 | bytes 4622592 | tf_op jit(solution)/shard_map/prcd,de->prce/dot_general | solution.py:48
  37.2 0.2 slice.58
  37.4 1.1 pad_maximum_fusion
  38.5 3.7 %reshape.311 = bf16[1,12,2,12,3,16,32]{6,5,4,3,2,1,0:T(8,128)(2,1)S(1)} reshape(bf16[1,12,24,1536]{3,2,1,0:T(8,128)(2,1)} %pad_maximum_fusion) | data formatting | bytes 1769472 | tf_op jit(solution)/shard_map/reshape | solution.py:53
  42.1 0.6 copy.26
  42.8 0.6 fusion.78
  43.4 1.7 copy.39
  45.1 1.0 copy.38
  46.2 1.0 copy.37
  47.2 4.0 %fusion.81 = (f32[2,16,144]{2,1,0:T(8,128)S(1)}, f32[2,16,144,144]{2,3,1,0:T(8,128)}) fusion(pred[2,144,144]{1,2,0:T(8,128)(4,1)S(1)} %copy-done.8, bf16[1,2,144,1,16,32]{2,5,4,1,3,0:T(8,128)(2,1)S(1)} %copy-done.7, bf16[1,2,144,1,16,32]{2,5,4,1,3,0:T(8,128)(2,1)S(1)} %copy.38), kind=kOutput, calls=%fused_computation.103 | convolution fusion | flops 45121680 | bytes 3303936 | tf_op jit(solution)/shard_map/sub | solution.py:75
  51.2 2.8 %fusion.23 = bf16[1,2,144,16,32]{2,4,3,1,0:T(8,128)(2,1)S(1)} fusion(f32[2,16,144,144]{2,3,1,0:T(8,128)} %get-tuple-element.33, f32[2,16,144]{2,1,0:T(8,128)S(1)} %get-tuple-element.32, bf16[1,2,144,1,16,32]{2,5,4,1,3,0:T(8,128)(2,1)S(1)} %copy.37), kind=kOutput, calls=%fused_computation.37 | convolution fusion | flops 43941888 | bytes 3262464 | tf_op jit(solution)/shard_map/pnhqk,pnkhd->pnqhd/dot_general | solution.py:77
  54.0 1.1 copy.31
  55.1 0.9 reshape.316
  56.0 0.1 copy.32
  56.0 0.1 reshape.317
  56.1 0.1 fusion.70
  56.2 1.8 collective-permute-start.1
  58.0 6.2 %collective-permute-done.1 = bf16[1,6,24,512]{3,2,1,0:T(8,128)(2,1)S(1)} collective-permute-done((bf16[1,6,24,512]{3,2,1,0:T(8,128)(2,1)S(1)}, bf16[1,6,24,512]{3,2,1,0:T(8,128)(2,1)S(1)}, u32[]{:S(2)}, u32[]{:S(2)}) %collective-permute-start.1) | collective-permute-done | bytes 147488 | tf_op jit(solution)/shard_map/ppermute | solution.py:13
  64.1 2.5 %fusion.20 = bf16[1,12,24,1024]{3,2,1,0:T(8,128)(2,1)} fusion(bf16[512,1024]{1,0:T(8,128)(2,1)} %all-gather.13.cloned.1.call-done, bf16[1,12,18,512]{3,2,1,0:T(8,128)(2,1)S(1)} %bitcast.99, bf16[1,12,6,512]{3,2,1,0:T(8,128)(2,1)S(1)} %slice.63, bf16[1,6,24,512]{3,2,1,0:T(8,128)(2,1)S(1)} %collective-permute-done.1), kind=kOutput, calls=%fused_computation.34 | convolution fusion | flops 303169536 | bytes 2080768 | tf_op jit(solution)/shard_map/prce,ed->prcd/dot_general | solution.py:85
  66.7 0.0 all-gather.15.cloned.1.call-start
  66.7 0.5 all-gather.15.cloned.1.call-update
  67.3 0.2 all-gather.21.cloned.1.call-start
  67.5 3.6 %copy.41 = bf16[128,8,2,512]{3,1,2,0:T(8,128)(2,1)} copy(bf16[128,8,2,512]{3,2,1,0:T(2,128)(2,1)} %bitcast.101) | data formatting | bytes 4194304
  71.1 25.1 %all-reduce.2.cloned.1.call-done = bf16[1,12,24,1024]{3,2,1,0:T(8,128)(2,1)} async-done(((bf16[1,12,24,1024]{3,2,1,0:T(8,128)(2,1)}), bf16[1,12,24,1024]{3,2,1,0:T(8,128)(2,1)}) %all-reduce.2.cloned.1.call-update) | async-done | bytes 589840 | tf_op jit(solution)/shard_map/psum | solution.py:88
  96.2 1.5 convert_reduce_fusion
  97.7 0.3 fusion.28
  98.0 0.2 fusion.29
  98.3 1.6 convolution_convert_fusion
  99.9 0.0 all-gather.19.cloned.1.call-start
  99.9 0.7 all-gather.19.cloned.1.call-update
  100.6 0.0 reduce-scatter.2.cloned.1.call-start
  100.7 0.1 convert_reduce_fusion.2
  100.8 0.3 fusion.34
  101.1 5.6 %all-gather.15.cloned.1.call-done = bf16[1024,512]{1,0:T(8,128)(2,1)} async-done(((bf16[512,512]{1,0:T(8,128)(2,1)}), bf16[1024,512]{1,0:T(8,128)(2,1)}) %all-gather.15.cloned.1.call-update) | async-done | bytes 1048592 | tf_op jit(solution)/shard_map/all_gather | solution.py:34
  106.8 1.7 convolution_convert_fusion.3
  108.5 0.8 copy.33
  109.3 50.8 %all-gather.21.cloned.1.call-done = bf16[1152,1024]{1,0:T(8,128)(2,1)} async-done(((bf16[288,1024]{1,0:T(8,128)(2,1)}), bf16[1152,1024]{1,0:T(8,128)(2,1)}) %all-gather.21.cloned.1.call-update) | async-done | bytes 2359312 | tf_op jit(solution)/shard_map/all_gather | solution.py:115
  160.1 1.8 fusion.79
  161.9 0.7 copy.34
  162.6 2.5 %multiply_reduce_fusion = (f32[8,256]{1,0:T(8,128)S(1)}, f32[8,256,1152]{2,1,0:T(8,128)S(1)}) fusion(bf16[256,8,64]{0,2,1:T(8,128)(2,1)} %bitcast.108, bf16[1152,8,64]{0,2,1:T(8,128)(2,1)S(1)} %bitcast.97), kind=kOutput, calls=%fused_computation.2 | convolution fusion | flops 306706432 | bytes 10887168 | tf_op jit(solution)/shard_map/while/body/eval_jaxpr/pqhd,pkhd->phqk/dot_general | solution.py:133
  165.1 1.9 fusion.1
  167.0 1.7 copy-done
  168.7 0.7 copy.35
  169.4 5.5 %fusion.40 = bf16[8,256,64]{1,2,0:T(8,128)(2,1)S(1)} fusion(bf16[1152,8,64]{0,2,1:T(8,128)(2,1)S(1)} %bitcast.105, f32[8,256,1152]{2,1,0:T(8,128)} %copy-done, f32[8,256]{1,0:T(8,128)S(1)} %get-tuple-element.34, f32[8,256]{1,0:T(8,128)S(1)} %get-tuple-element.31, f32[8,256]{1,0:T(8,128)S(1)} %get-tuple-element.30), kind=kOutput, calls=%fused_computation.52 | convolution fusion | flops 309460992 | bytes 10903552 | tf_op jit(solution)/shard_map/while/body/eval_jaxpr/phqk,pkhd->phqd/dot_general | solution.py:140
  175.0 2.5 %fusion.24 = bf16[256,1,1024]{2,0,1:T(8,128)(2,1)} fusion(bf16[256,512]{0,1:T(8,128)(2,1)S(1)} %bitcast.110, bf16[512,1024]{1,0:T(8,128)(2,1)} %all-gather.19.cloned.1.call-done), kind=kOutput, calls=%fused_computation.38 | convolution fusion | flops 268697600 | bytes 1835008 | tf_op jit(solution)/shard_map/pte,ed->tpd/dot_general | solution.py:157
  177.6 13.6 %reduce-scatter.2.cloned.1.call-done = bf16[128,1,1024]{2,0,1:T(8,128)(2,1)} async-done(((bf16[256,1,1024]{2,0,1:T(8,128)(2,1)}), bf16[128,1,1024]{2,0,1:T(8,128)(2,1)}) %reduce-scatter.2.cloned.1.call-update) | async-done | bytes 262160 | tf_op jit(solution)/shard_map/reduce_scatter | solution.py:156
  191.2 1.7 fusion.50
  (40 shorter events, 0.4 us)
Async XLA Ops:
  7.2 2.3 %copy-start.4 = (bf16[1,12,24,1024]{3,2,1,0:T(8,128)(2,1)S(1)}, bf16[1,12,24,1024]{3,2,1,0:T(8,128)(2,1)}, u32[]{:S(2)}) copy-start(bf16[1,12,24,1024]{3,2,1,0:T(8,128)(2,1)} %param.8) | copy-start | bytes 1769476
  7.2 15.8 %all-gather.11.cloned.1.call-start = ((), (), s32[]{:S(2)}) async-start(), calls=%async_computation.2 | async-start | bytes 3145728 | tf_op jit(solution)/shard_map/all_gather | solution.py:32
  7.9 26.8 %all-gather.9.cloned.1.call-start = ((), (), s32[]{:S(2)}) async-start(), calls=%async_computation.1 | async-start | bytes 1572864 | tf_op jit(solution)/shard_map/all_gather | solution.py:31
  8.7 49.3 %all-gather.13.cloned.1.call-start = ((), (), s32[]{:S(2)}) async-start(), calls=%async_computation.3 | async-start | bytes 1572864 | tf_op jit(solution)/shard_map/all_gather | solution.py:33
  9.4 58.1 %all-gather.17.cloned.1.call-start = ((), (), s32[]{:S(2)}) async-start(), calls=%async_computation.6 | async-start | bytes 3145728 | tf_op jit(solution)/shard_map/all_gather | solution.py:35
  9.6 11.4 %collective-permute-start = (bf16[1,6,24,1024]{3,2,1,0:T(8,128)(2,1)S(1)}, bf16[1,6,24,1024]{3,2,1,0:T(8,128)(2,1)S(1)}, u32[]{:S(2)}, u32[]{:S(2)}) collective-permute-start(bf16[1,6,24,1024]{3,2,1,0:T(8,128)(2,1)S(1)} %get-tuple-element.29), channel_id=1, source_target_pairs={{0,12},{4,0},{8,4},{12,8},{1,13},{5,1},{9,5},{13,9},{2,14},{6,2},{... | collective-permute-start | bytes 884744 | tf_op jit(solution)/shard_map/ppermute | solution.py:13
  14.7 81.5 %all-reduce.2.cloned.1.call-start = ((), (), s32[]{:S(2)}) async-start(), calls=%async_computation.4 | async-start | bytes 1179648 | tf_op jit(solution)/shard_map/psum | solution.py:88
  45.1 2.1 %copy-start.7 = (bf16[1,2,144,1,16,32]{2,5,4,1,3,0:T(8,128)(2,1)S(1)}, bf16[1,2,144,1,16,32]{2,5,4,1,3,0:T(8,128)(2,1)}, u32[]{:S(2)}) copy-start(bf16[1,2,144,1,16,32]{2,5,4,1,3,0:T(8,128)(2,1)} %copy.39) | copy-start | bytes 884740
  45.1 2.1 %copy-start.8 = (pred[2,144,144]{1,2,0:T(8,128)(4,1)S(1)}, pred[2,144,144]{1,2,0:T(8,128)(4,1)}, u32[]{:S(2)}) copy-start(pred[2,144,144]{1,2,0:T(8,128)(4,1)} %broadcast_compare_fusion) | copy-start | bytes 124420
  56.2 8.0 %collective-permute-start.1 = (bf16[1,6,24,512]{3,2,1,0:T(8,128)(2,1)S(1)}, bf16[1,6,24,512]{3,2,1,0:T(8,128)(2,1)S(1)}, u32[]{:S(2)}, u32[]{:S(2)}) collective-permute-start(bf16[1,6,24,512]{3,2,1,0:T(8,128)(2,1)S(1)} %fusion.70), channel_id=1, source_target_pairs={{0,4},{4,8},{8,12},{12,0},{1,5},{5,9},{9,13},{13,1},{2,6},{6,10},{... | collective-permute-start | bytes 442376 | tf_op jit(solution)/shard_map/ppermute | solution.py:13
  66.7 40.1 %all-gather.15.cloned.1.call-start = ((), (), s32[]{:S(2)}) async-start(), calls=%async_computation.5 | async-start | bytes 1572864 | tf_op jit(solution)/shard_map/all_gather | solution.py:34
  67.3 92.8 %all-gather.21.cloned.1.call-start = ((), (), s32[]{:S(2)}) async-start(), calls=%async_computation.9 | async-start | bytes 2949120 | tf_op jit(solution)/shard_map/all_gather | solution.py:115
  67.5 28.7 %copy-start.5 = (bf16[1,12,24,1024]{3,2,1,0:T(8,128)(2,1)S(1)}, bf16[1,12,24,1024]{3,2,1,0:T(8,128)(2,1)}, u32[]{:S(2)}) copy-start(bf16[1,12,24,1024]{3,2,1,0:T(8,128)(2,1)} %param.8) | copy-start | bytes 1769476
  96.2 2.0 %copy-start.6 = (bf16[128,8,2,512]{3,1,2,0:T(8,128)(2,1)S(1)}, bf16[128,8,2,512]{3,1,2,0:T(8,128)(2,1)}, u32[]{:S(2)}) copy-start(bf16[128,8,2,512]{3,1,2,0:T(8,128)(2,1)} %copy.41) | copy-start | bytes 6291460
  97.7 2.2 %copy-start.1 = (bf16[1,12,24,1024]{3,2,1,0:T(8,128)(2,1)}, bf16[1,12,24,1024]{3,2,1,0:T(8,128)(2,1)S(1)}, u32[]{:S(2)}) copy-start(bf16[1,12,24,1024]{3,2,1,0:T(8,128)(2,1)S(1)} %get-tuple-element.15) | copy-start | bytes 1769476
  98.2 2.4 %copy-start.2 = (bf16[1,256,1024]{2,1,0:T(8,128)(2,1)S(1)}, bf16[1,256,1024]{2,1,0:T(8,128)(2,1)}, u32[]{:S(2)}) copy-start(bf16[1,256,1024]{2,1,0:T(8,128)(2,1)} %param.9) | copy-start | bytes 1572868
  99.9 75.1 %all-gather.19.cloned.1.call-start = ((), (), s32[]{:S(2)}) async-start(), calls=%async_computation.7 | async-start | bytes 1572864 | tf_op jit(solution)/shard_map/all_gather | solution.py:36
  100.6 90.6 %reduce-scatter.2.cloned.1.call-start = ((), (), s32[]{:S(2)}) async-start(), calls=%async_computation.8 | async-start | bytes 786432 | tf_op jit(solution)/shard_map/reduce_scatter | solution.py:156
  165.1 3.7 %copy-start = (f32[8,256,1152]{2,1,0:T(8,128)}, f32[8,256,1152]{2,1,0:T(8,128)S(1)}, u32[]{:S(2)}) copy-start(f32[8,256,1152]{2,1,0:T(8,128)S(1)} %get-tuple-element.35) | copy-start | bytes 28311556
  175.0 16.3 %copy-start.3 = (bf16[1,256,1024]{2,1,0:T(8,128)(2,1)S(1)}, bf16[1,256,1024]{2,1,0:T(8,128)(2,1)}, u32[]{:S(2)}) copy-start(bf16[1,256,1024]{2,1,0:T(8,128)(2,1)} %param.9) | copy-start | bytes 1572868
Sparse Core Ops, SparseCore 0:
  9.6 13.3 all-gather.10
  24.5 10.1 all-gather.8
  36.3 10.1 all-gather.12
  47.9 11.7 all-gather.16
  66.8 29.3 all-reduce.1
  97.7 9.0 all-gather.14
  108.4 51.6 all-gather.20
  161.7 7.8 all-gather.18
  177.7 13.4 reduce-scatter.1
where the time goes:
time: 200 us; the launch traced here: 199 us
  waiting for transfers between devices  121 us (60%)
  matrix products  25.6 us (13%)
  local copies, waits for them, and re-layouts  22.9 us (11%)
  between operations  14.2 us (7%)
  other arithmetic  8.42 us (4%)
  starting transfers between devices  7.43 us (4%)
    all_gather x1, waiting for transfers between devices, body(): shard_rows = lax.all_gather(page_kv, 'tile', axis=1, tiled=True)  50.8 us
    psum x1, waiting for transfers between devices, body(): lax.psum(partial_proj.astype(jnp.bfloat16), 'mp').astype(jnp.float32)  25.1 us
    reduce_scatter x1, waiting for transfers between devices, body(): lax.psum_scatter(jnp.einsum('pte,ed->tpd', context, wout_dec, preferred_e...  13.6 us
    ppermute x2, waiting for transfers between devices, from_behind(): lax.ppermute(value, axis, [(i, (i + by) % devices) for i in range(devices)])  11.3 us
    unnamed x23, local copies, waits for them, and re-layouts  11.3 us
    all_gather x1, waiting for transfers between devices, body(): lax.all_gather(enc_query, 'batch', axis=0, tiled=True)  9.63 us
    ppermute x2, starting transfers between devices, from_behind(): lax.ppermute(value, axis, [(i, (i + by) % devices) for i in range(devices)])  6.9 us
    all_gather x1, waiting for transfers between devices, body(): lax.all_gather(dec_query, 'batch', axis=0, tiled=True)  5.6 us
  transfers between devices with their start and end apart: 11, of which 8 were waited for; matrix products, arithmetic and copies ran while one was open for 25% of the time, Pallas kernels for 0%

commit v1 on v0

--- a/solution.py
+++ b/solution.py
@@ -112,7 +112,12 @@
         jnp.zeros((pages_here, heads_dec, text_len, HEAD_DEC), jnp.float32),
     )
     carried = start_state
-    shard_rows = lax.all_gather(page_kv, "tile", axis=1, tiled=True)
+    ring = [page_kv]
+    for hop in range(3):
+        ring.append(lax.ppermute(ring[-1], "tile", [(dev, (dev + 1) % 4) for dev in range(4)]))
+    shard_rows = jnp.roll(
+        jnp.concatenate(ring[::-1], axis=1), (lax.axis_index("tile") + 1) * ring[0].shape[1], axis=1
+    )
     count = shard_rows.shape[1] // own_rows
     grouped = max(
         (

time: 200 us -> 186 us (0.930)
  waiting for transfers between devices: 121 us -> 104 us
    all_gather x1 -> x0, waiting for transfers between devices: 50.8 us -> none  [body(): shard_rows = lax.all_gather(page_kv, 'tile', axis=1, tiled=True)]
    ppermute x0 -> x3, waiting for transfers between devices: none -> 43.3 us  [body(): lax.ppermute(ring[-1], 'tile', [(dev, (dev + 1) % 4) for dev in range(4)])]
    all_gather x1, waiting for transfers between devices: 5.6 us -> 0.02 us  [body(): lax.all_gather(dec_query, 'batch', axis=0, tiled=True)]
    unnamed x23 -> x24, local copies, waits for them, and re-layouts: 11.3 us -> 11.5 us
  transfers between devices with their start and end apart: 11 -> 13, of which waited for: 8 -> 9; matrix products, arithmetic and copies ran while one was open for 25% -> 28% of each run, Pallas kernels for 0% -> 0%
where the time goes in v1:
time: 186 us
  waiting for transfers between devices  104 us (56%)
  matrix products  25.8 us (14%)
  local copies, waits for them, and re-layouts  23.3 us (13%)
  between operations  14.6 us (8%)
  starting transfers between devices  8.94 us (5%)
  other arithmetic  8.39 us (5%)
    ppermute x3, waiting for transfers between devices, body(): lax.ppermute(ring[-1], 'tile', [(dev, (dev + 1) % 4) for dev in range(4)])  43.3 us
    psum x1, waiting for transfers between devices, body(): lax.psum(partial_proj.astype(jnp.bfloat16), 'mp').astype(jnp.float32)  25.2 us
    reduce_scatter x1, waiting for transfers between devices, body(): lax.psum_scatter(jnp.einsum('pte,ed->tpd', context, wout_dec, preferred_e...  12 us
    unnamed x24, local copies, waits for them, and re-layouts  11.5 us
    ppermute x2, waiting for transfers between devices, from_behind(): lax.ppermute(value, axis, [(i, (i + by) % devices) for i in range(devices)])  11.3 us
    all_gather x1, waiting for transfers between devices, body(): lax.all_gather(enc_query, 'batch', axis=0, tiled=True)  9.63 us
    ppermute x2, starting transfers between devices, from_behind(): lax.ppermute(value, axis, [(i, (i + by) % devices) for i in range(devices)])  6.9 us
    dot_general x1, matrix products, advance(): jnp.einsum('phqk,pkhd->phqd', expo.astype(jnp.bfloat16), block_vals, pref...  5.57 us
  transfers between devices with their start and end apart: 13, of which 9 were waited for; matrix products, arithmetic and copies ran while one was open for 28% of the time, Pallas kernels for 0%

profile of v1, /device:TPU:0, one launch (start us, length us, event | category | flops | bytes accessed | tf_op | source)
XLA Modules:
  0.0 185.5 jit_solution(990386761072446259)
XLA Ops:
  7.2 0.7 all-gather.9.cloned.1.call-update
  7.9 0.0 all-gather.7.cloned.1.call-start
  7.9 0.7 all-gather.7.cloned.1.call-update
  8.7 0.7 all-gather.11.cloned.1.call-update
  9.4 1.2 fusion.80
  10.6 5.1 %collective-permute-start = (bf16[1,6,24,1024]{3,2,1,0:T(8,128)(2,1)S(1)}, bf16[1,6,24,1024]{3,2,1,0:T(8,128)(2,1)S(1)}, u32[]{:S(2)}, u32[]{:S(2)}) collective-permute-start(bf16[1,6,24,1024]{3,2,1,0:T(8,128)(2,1)S(1)} %get-tuple-element.29), channel_id=1, source_target_pairs={{0,12},{4,0},{8,4},{12,8},{1,13},{5,1},{9,5},{13,9},{2,14},{6,2},{... | collective-permute-start | bytes 884744 | tf_op jit(solution)/shard_map/ppermute | solution.py:13
  15.7 0.0 all-reduce.2.cloned.1.call-start
  15.8 0.1 add.99
  15.9 0.1 add.95
  16.0 0.1 add.96
  16.1 0.7 broadcast_compare_fusion
  16.8 5.1 %collective-permute-done = bf16[1,6,24,1024]{3,2,1,0:T(8,128)(2,1)S(1)} collective-permute-done((bf16[1,6,24,1024]{3,2,1,0:T(8,128)(2,1)S(1)}, bf16[1,6,24,1024]{3,2,1,0:T(8,128)(2,1)S(1)}, u32[]{:S(2)}, u32[]{:S(2)}) %collective-permute-start) | collective-permute-done | bytes 294944 | tf_op jit(solution)/shard_map/ppermute | solution.py:13
  22.0 0.1 convert_reduce_fusion.1
  22.1 0.3 fusion.32
  22.4 0.4 all-gather.9.cloned.1.call-done
  22.9 2.1 %copy.40 = bf16[128,8,2,512]{3,1,2,0:T(8,128)(2,1)S(1)} copy(bf16[128,8,2,512]{3,2,1,0:T(2,128)(2,1)} %bitcast.102) | data formatting | bytes 4194304
  25.0 9.6 %all-gather.7.cloned.1.call-done = bf16[1024,512]{1,0:T(8,128)(2,1)} async-done(((bf16[512,512]{1,0:T(8,128)(2,1)}), bf16[1024,512]{1,0:T(8,128)(2,1)}) %all-gather.7.cloned.1.call-update) | async-done | bytes 1048592 | tf_op jit(solution)/shard_map/all_gather | solution.py:31
  34.6 2.4 %fusion.12 = bf16[1,12,24,1536]{3,2,1,0:T(8,128)(2,1)S(1)} fusion(bf16[1024,1024]{1,0:T(8,128)(2,1)S(1)} %bitcast.104, bf16[1024,512]{1,0:T(8,128)(2,1)} %all-gather.7.cloned.1.call-done, bf16[6,24,1024]{2,1,0:T(8,128)(2,1)S(1)} %bitcast.106, bf16[6,24,1024]{2,1,0:T(8,128)(2,1)S(1)} %get-tuple-element.28, f32[12,24]{1,0:T(8,128)S(1)} %add_sqrt_fusion.1, ...), kind=kOutput, calls=%fused_computation.17 | convolution fusion | flops 914178048 | bytes 4622592 | tf_op jit(solution)/shard_map/prcd,de->prce/dot_general | solution.py:48
  37.1 0.2 slice.58
  37.3 1.1 pad_maximum_fusion
  38.4 3.7 %reshape.311 = bf16[1,12,2,12,3,16,32]{6,5,4,3,2,1,0:T(8,128)(2,1)S(1)} reshape(bf16[1,12,24,1536]{3,2,1,0:T(8,128)(2,1)} %pad_maximum_fusion) | data formatting | bytes 1769472 | tf_op jit(solution)/shard_map/reshape | solution.py:53
  42.0 0.6 copy.26
  42.7 0.6 fusion.79
  43.3 1.7 copy.39
  45.0 1.0 copy.38
  46.1 1.0 copy.37
  47.1 5.0 %fusion.81 = (f32[2,16,144]{2,1,0:T(8,128)S(1)}, f32[2,16,144,144]{2,3,1,0:T(8,128)}) fusion(pred[2,144,144]{1,2,0:T(8,128)(4,1)} %broadcast_compare_fusion, bf16[1,2,144,1,16,32]{2,5,4,1,3,0:T(8,128)(2,1)} %copy.39, bf16[1,2,144,1,16,32]{2,5,4,1,3,0:T(8,128)(2,1)S(1)} %copy.38), kind=kOutput, calls=%fused_computation.113 | convolution fusion | flops 45121680 | bytes 3303936 | tf_op jit(solution)/shard_map/sub | solution.py:75
  52.1 2.8 %fusion.24 = bf16[1,2,144,16,32]{2,4,3,1,0:T(8,128)(2,1)S(1)} fusion(f32[2,16,144,144]{2,3,1,0:T(8,128)} %get-tuple-element.33, f32[2,16,144]{2,1,0:T(8,128)S(1)} %get-tuple-element.32, bf16[1,2,144,1,16,32]{2,5,4,1,3,0:T(8,128)(2,1)S(1)} %copy.37), kind=kOutput, calls=%fused_computation.38 | convolution fusion | flops 43941888 | bytes 3262464 | tf_op jit(solution)/shard_map/pnhqk,pnkhd->pnqhd/dot_general | solution.py:77
  54.9 1.1 copy.31
  56.0 0.9 reshape.316
  56.9 0.1 copy.32
  56.9 0.1 reshape.317
  57.0 0.1 fusion.71
  57.1 1.8 collective-permute-start.1
  58.9 6.2 %collective-permute-done.1 = bf16[1,6,24,512]{3,2,1,0:T(8,128)(2,1)S(1)} collective-permute-done((bf16[1,6,24,512]{3,2,1,0:T(8,128)(2,1)S(1)}, bf16[1,6,24,512]{3,2,1,0:T(8,128)(2,1)S(1)}, u32[]{:S(2)}, u32[]{:S(2)}) %collective-permute-start.1) | collective-permute-done | bytes 147488 | tf_op jit(solution)/shard_map/ppermute | solution.py:13
  65.1 2.5 %fusion.20 = bf16[1,12,24,1024]{3,2,1,0:T(8,128)(2,1)} fusion(bf16[512,1024]{1,0:T(8,128)(2,1)} %all-gather.11.cloned.1.call-done, bf16[1,12,18,512]{3,2,1,0:T(8,128)(2,1)S(1)} %bitcast.100, bf16[1,12,6,512]{3,2,1,0:T(8,128)(2,1)S(1)} %slice.63, bf16[1,6,24,512]{3,2,1,0:T(8,128)(2,1)S(1)} %collective-permute-done.1), kind=kOutput, calls=%fused_computation.34 | convolution fusion | flops 303169536 | bytes 2080768 | tf_op jit(solution)/shard_map/prce,ed->prcd/dot_general | solution.py:85
  67.6 0.0 all-gather.13.cloned.1.call-start
  67.7 0.5 all-gather.13.cloned.1.call-update
  68.2 0.2 all-gather.17.cloned.1.call-start
  68.5 3.5 %copy.41 = bf16[128,8,2,512]{3,1,2,0:T(8,128)(2,1)} copy(bf16[128,8,2,512]{3,2,1,0:T(2,128)(2,1)} %bitcast.101) | data formatting | bytes 4194304
  72.0 25.2 %all-reduce.2.cloned.1.call-done = bf16[1,12,24,1024]{3,2,1,0:T(8,128)(2,1)} async-done(((bf16[1,12,24,1024]{3,2,1,0:T(8,128)(2,1)}), bf16[1,12,24,1024]{3,2,1,0:T(8,128)(2,1)}) %all-reduce.2.cloned.1.call-update) | async-done | bytes 589840 | tf_op jit(solution)/shard_map/psum | solution.py:88
  97.1 1.5 convert_reduce_fusion
  98.6 0.3 fusion.29
  98.9 0.2 fusion.30
  99.2 0.8 fusion.21
  100.0 1.5 collective-permute-start.2
  101.5 15.4 %collective-permute-done.2 = bf16[1,288,1024]{2,1,0:T(8,128)(2,1)S(1)} collective-permute-done((bf16[1,288,1024]{2,1,0:T(8,128)(2,1)S(1)}, bf16[1,288,1024]{2,1,0:T(8,128)(2,1)S(1)}, u32[]{:S(2)}, u32[]{:S(2)}) %collective-permute-start.2) | collective-permute-done | bytes 589856 | tf_op jit(solution)/shard_map/ppermute | solution.py:117
  116.9 0.0 reduce-scatter.2.cloned.1.call-start
  117.0 0.1 convert_reduce_fusion.2
  117.1 15.7 %collective-permute-done.3 = bf16[1,288,1024]{2,1,0:T(8,128)(2,1)S(1)} collective-permute-done((bf16[1,288,1024]{2,1,0:T(8,128)(2,1)S(1)}, bf16[1,288,1024]{2,1,0:T(8,128)(2,1)S(1)}, u32[]{:S(2)}, u32[]{:S(2)}) %collective-permute-start.3) | collective-permute-done | bytes 589856 | tf_op jit(solution)/shard_map/ppermute | solution.py:117
  132.9 0.3 fusion.35
  133.2 1.7 convolution_convert_fusion.3
  135.0 0.8 copy.33
  135.8 12.2 %collective-permute-done.4 = bf16[1,288,1024]{2,1,0:T(8,128)(2,1)S(1)} collective-permute-done((bf16[1,288,1024]{2,1,0:T(8,128)(2,1)S(1)}, bf16[1,288,1024]{2,1,0:T(8,128)(2,1)S(1)}, u32[]{:S(2)}, u32[]{:S(2)}) %collective-permute-start.4) | collective-permute-done | bytes 589856 | tf_op jit(solution)/shard_map/ppermute | solution.py:117
  148.3 1.0 constant_dynamic-slice_fusion
  149.3 0.7 copy.34
  150.0 2.5 %multiply_reduce_fusion = (f32[8,256]{1,0:T(8,128)S(1)}, f32[8,256,1152]{2,1,0:T(8,128)S(1)}) fusion(bf16[256,8,64]{0,2,1:T(8,128)(2,1)} %bitcast.108, bf16[1152,8,64]{0,2,1:T(8,128)(2,1)S(1)} %bitcast.98), kind=kOutput, calls=%fused_computation.2 | convolution fusion | flops 306706432 | bytes 10887168 | tf_op jit(solution)/shard_map/while/body/eval_jaxpr/pqhd,pkhd->phqk/dot_general | solution.py:138
  152.5 1.9 %fusion.1 = f32[8,256]{1,0:T(8,128)S(1)} fusion(f32[8,256,1152]{2,1,0:T(8,128)S(1)} %get-tuple-element.35, f32[8,256]{1,0:T(8,128)S(1)} %get-tuple-element.34), kind=kLoop, calls=%fused_computation.3 | loop fusion | flops 7075840 | bytes 9453568 | tf_op jit(solution)/shard_map/while/body/eval_jaxpr/reduce_sum | solution.py:144
  154.4 1.7 copy-done
  156.1 0.7 copy.35
  156.9 5.6 %fusion.41 = bf16[8,256,64]{1,2,0:T(8,128)(2,1)S(1)} fusion(bf16[1152,8,64]{0,2,1:T(8,128)(2,1)S(1)} %bitcast.105, f32[8,256,1152]{2,1,0:T(8,128)} %copy-done, f32[8,256]{1,0:T(8,128)S(1)} %get-tuple-element.34, f32[8,256]{1,0:T(8,128)S(1)} %get-tuple-element.31, f32[8,256]{1,0:T(8,128)S(1)} %get-tuple-element.30), kind=kOutput, calls=%fused_computation.53 | convolution fusion | flops 309460992 | bytes 10903552 | tf_op jit(solution)/shard_map/while/body/eval_jaxpr/phqk,pkhd->phqd/dot_general | solution.py:145
  162.5 2.5 %fusion.25 = bf16[256,1,1024]{2,0,1:T(8,128)(2,1)} fusion(bf16[256,512]{0,1:T(8,128)(2,1)S(1)} %bitcast.110, bf16[512,1024]{1,0:T(8,128)(2,1)} %all-gather.17.cloned.1.call-done), kind=kOutput, calls=%fused_computation.39 | convolution fusion | flops 268697600 | bytes 1835008 | tf_op jit(solution)/shard_map/pte,ed->tpd/dot_general | solution.py:162
  165.0 12.0 %reduce-scatter.2.cloned.1.call-done = bf16[128,1,1024]{2,0,1:T(8,128)(2,1)} async-done(((bf16[256,1,1024]{2,0,1:T(8,128)(2,1)}), bf16[128,1,1024]{2,0,1:T(8,128)(2,1)}) %reduce-scatter.2.cloned.1.call-update) | async-done | bytes 262160 | tf_op jit(solution)/shard_map/reduce_scatter | solution.py:161
  177.0 1.7 fusion.51
  (45 shorter events, 0.7 us)
Async XLA Ops:
  7.2 15.7 %all-gather.9.cloned.1.call-start = ((), (), s32[]{:S(2)}) async-start(), calls=%async_computation.2 | async-start | bytes 3145728 | tf_op jit(solution)/shard_map/all_gather | solution.py:32
  7.9 26.7 %all-gather.7.cloned.1.call-start = ((), (), s32[]{:S(2)}) async-start(), calls=%async_computation.1 | async-start | bytes 1572864 | tf_op jit(solution)/shard_map/all_gather | solution.py:31
  8.6 50.3 %all-gather.11.cloned.1.call-start = ((), (), s32[]{:S(2)}) async-start(), calls=%async_computation.3 | async-start | bytes 1572864 | tf_op jit(solution)/shard_map/all_gather | solution.py:33
  9.4 59.1 %all-gather.15.cloned.1.call-start = ((), (), s32[]{:S(2)}) async-start(), calls=%async_computation.6 | async-start | bytes 3145728 | tf_op jit(solution)/shard_map/all_gather | solution.py:35
  10.6 11.4 %collective-permute-start = (bf16[1,6,24,1024]{3,2,1,0:T(8,128)(2,1)S(1)}, bf16[1,6,24,1024]{3,2,1,0:T(8,128)(2,1)S(1)}, u32[]{:S(2)}, u32[]{:S(2)}) collective-permute-start(bf16[1,6,24,1024]{3,2,1,0:T(8,128)(2,1)S(1)} %get-tuple-element.29), channel_id=1, source_target_pairs={{0,12},{4,0},{8,4},{12,8},{1,13},{5,1},{9,5},{13,9},{2,14},{6,2},{... | collective-permute-start | bytes 884744 | tf_op jit(solution)/shard_map/ppermute | solution.py:13
  15.7 81.4 %all-reduce.2.cloned.1.call-start = ((), (), s32[]{:S(2)}) async-start(), calls=%async_computation.4 | async-start | bytes 1179648 | tf_op jit(solution)/shard_map/psum | solution.py:88
  57.1 40.0 %copy-start.4 = (bf16[1,12,24,1024]{3,2,1,0:T(8,128)(2,1)S(1)}, bf16[1,12,24,1024]{3,2,1,0:T(8,128)(2,1)}, u32[]{:S(2)}) copy-start(bf16[1,12,24,1024]{3,2,1,0:T(8,128)(2,1)} %param.8) | copy-start | bytes 1769476
  57.1 8.0 %collective-permute-start.1 = (bf16[1,6,24,512]{3,2,1,0:T(8,128)(2,1)S(1)}, bf16[1,6,24,512]{3,2,1,0:T(8,128)(2,1)S(1)}, u32[]{:S(2)}, u32[]{:S(2)}) collective-permute-start(bf16[1,6,24,512]{3,2,1,0:T(8,128)(2,1)S(1)} %fusion.71), channel_id=1, source_target_pairs={{0,4},{4,8},{8,12},{12,0},{1,5},{5,9},{9,13},{13,1},{2,6},{6,10},{... | collective-permute-start | bytes 442376 | tf_op jit(solution)/shard_map/ppermute | solution.py:13
  67.6 65.6 %all-gather.13.cloned.1.call-start = ((), (), s32[]{:S(2)}) async-start(), calls=%async_computation.5 | async-start | bytes 1572864 | tf_op jit(solution)/shard_map/all_gather | solution.py:34
  68.2 94.3 %all-gather.17.cloned.1.call-start = ((), (), s32[]{:S(2)}) async-start(), calls=%async_computation.7 | async-start | bytes 1572864 | tf_op jit(solution)/shard_map/all_gather | solution.py:36
  97.1 2.0 %copy-start.5 = (bf16[128,8,2,512]{3,1,2,0:T(8,128)(2,1)S(1)}, bf16[128,8,2,512]{3,1,2,0:T(8,128)(2,1)}, u32[]{:S(2)}) copy-start(bf16[128,8,2,512]{3,1,2,0:T(8,128)(2,1)} %copy.41) | copy-start | bytes 6291460
  98.6 18.3 %copy-start.1 = (bf16[1,12,24,1024]{3,2,1,0:T(8,128)(2,1)}, bf16[1,12,24,1024]{3,2,1,0:T(8,128)(2,1)S(1)}, u32[]{:S(2)}) copy-start(bf16[1,12,24,1024]{3,2,1,0:T(8,128)(2,1)S(1)} %get-tuple-element.15) | copy-start | bytes 1769476
  98.9 18.1 %copy-start.2 = (bf16[1,256,1024]{2,1,0:T(8,128)(2,1)S(1)}, bf16[1,256,1024]{2,1,0:T(8,128)(2,1)}, u32[]{:S(2)}) copy-start(bf16[1,256,1024]{2,1,0:T(8,128)(2,1)} %param.9) | copy-start | bytes 1572868
  100.0 16.9 %collective-permute-start.2 = (bf16[1,288,1024]{2,1,0:T(8,128)(2,1)S(1)}, bf16[1,288,1024]{2,1,0:T(8,128)(2,1)S(1)}, u32[]{:S(2)}, u32[]{:S(2)}) collective-permute-start(bf16[1,288,1024]{2,1,0:T(8,128)(2,1)S(1)} %fusion.21), channel_id=1, source_target_pairs={{0,4},{4,8},{8,12},{12,0},{1,5},{5,9},{9,13},{13,1},{2,6},{6,10},{... | collective-permute-start | bytes 1769480 | tf_op jit(solution)/shard_map/ppermute | solution.py:117
  116.9 16.0 %collective-permute-start.3 = (bf16[1,288,1024]{2,1,0:T(8,128)(2,1)S(1)}, bf16[1,288,1024]{2,1,0:T(8,128)(2,1)S(1)}, u32[]{:S(2)}, u32[]{:S(2)}) collective-permute-start(bf16[1,288,1024]{2,1,0:T(8,128)(2,1)S(1)} %collective-permute-done.2), channel_id=1, source_target_pairs={{0,4},{4,8},{8,12},{12,0},{1,5},{5,9},{9,13},{13,1},{2,6},{6,10},{... | collective-permute-start | bytes 1769480 | tf_op jit(solution)/shard_map/ppermute | solution.py:117
  116.9 60.0 %reduce-scatter.2.cloned.1.call-start = ((), (), s32[]{:S(2)}) async-start(), calls=%async_computation.8 | async-start | bytes 786432 | tf_op jit(solution)/shard_map/reduce_scatter | solution.py:161
  132.9 15.1 %collective-permute-start.4 = (bf16[1,288,1024]{2,1,0:T(8,128)(2,1)S(1)}, bf16[1,288,1024]{2,1,0:T(8,128)(2,1)S(1)}, u32[]{:S(2)}, u32[]{:S(2)}) collective-permute-start(bf16[1,288,1024]{2,1,0:T(8,128)(2,1)S(1)} %collective-permute-done.3), channel_id=1, source_target_pairs={{0,4},{4,8},{8,12},{12,0},{1,5},{5,9},{9,13},{13,1},{2,6},{6,10},{... | collective-permute-start | bytes 1769480 | tf_op jit(solution)/shard_map/ppermute | solution.py:117
  152.5 3.6 %copy-start = (f32[8,256,1152]{2,1,0:T(8,128)}, f32[8,256,1152]{2,1,0:T(8,128)S(1)}, u32[]{:S(2)}) copy-start(f32[8,256,1152]{2,1,0:T(8,128)S(1)} %get-tuple-element.35) | copy-start | bytes 28311556
  156.9 20.1 %copy-start.3 = (bf16[1,256,1024]{2,1,0:T(8,128)(2,1)S(1)}, bf16[1,256,1024]{2,1,0:T(8,128)(2,1)}, u32[]{:S(2)}) copy-start(bf16[1,256,1024]{2,1,0:T(8,128)(2,1)} %param.9) | copy-start | bytes 1572868
Sparse Core Ops, SparseCore 0:
  9.5 13.2 all-gather.8
  24.4 10.1 all-gather.6
  36.2 10.1 all-gather.10
  47.8 11.7 all-gather.14
  67.7 29.3 all-reduce.1
  98.6 9.0 all-gather.12
  117.0 9.5 all-gather.16
  165.1 11.7 reduce-scatter.1
